TPU v7x, 32 devices: a whole 2x2x4 slice. The times are simulated.
32 devices in a mesh: tile: 8 (over z, y), clip: 4 (over x, core).
Axes of the slice: x: 2, y: 2, z: 4, core: 2. Of those that a mesh axis runs over, the one named last changes fastest.
Arguments:
- seq_rows: bfloat16 [32768, 512], P(('tile', 'clip'))
- plan_owner: int32 [32768], P(('tile', 'clip')), may hold values from 0 to 31, as said below
- plan_slot: int32 [32768], P(('tile', 'clip')), may hold values from 0 to 1023, as said below
- live_frames: int32 [4], replicated, may hold values from 1 to 4, as said below
- norm_gain: float32 [512], replicated, may hold values from 0.1 to 1.9
- norm_bias: float32 [512], replicated, may hold values from -3 to 3
- conv_weight: bfloat16 [3, 3, 512, 3, 256], replicated, may hold values from -0.0546875 to 0.0546875
- conv_bias: float32 [256], replicated, may hold values from -3 to 3
Outputs:
- decoded: bfloat16 [4, 8, 4, 8, 32, 256], P('clip', 'tile')
Inputs may be any that keep to these rules, and one draw needn't show every extreme that they name: `plan_owner`: owner o is tile o % 8 of clip o // 8. The 1024 rows of each device send 32 // 2 or 48 rows to each owner, so at most 48, which is reached. The pairs of plan_owner and plan_slot are all distinct: every slot of every owner receives exactly one row. `live_frames`: some clip has all 4 frames live.
All inputs are finite; a program needn't handle non-finite values.
Results may differ from a plain program's by a relative error of at most 0.004.
Values may be sent and summed in bfloat16 or wider, within the bound.
A program may use at most 128 MiB of HBM per device.

v0:
```python
import jax
import jax.numpy as jnp
from jax import lax
from jax.sharding import PartitionSpec as P

GROUPS = 32
LT = 4
TH = 8
TW = 32
GW = 4
EPSILON = 1e-06
HIGHEST = lax.Precision.HIGHEST


def shifted(block, axis, distance):
    devices = range(lax.axis_size(axis))
    route = [(i - distance, i) for i in devices if i - distance in devices]
    return lax.ppermute(block, axis, route)


def neighbour(values, offset):
    return shifted(values, "tile", offset)


def extend(tile_grid, column_tile, grid_cols):
    left_face = neighbour(tile_grid[:, :, -1:], 1)
    right_face = neighbour(tile_grid[:, :, :1], -1)
    left_face = jnp.where(column_tile > 0, left_face, jnp.zeros_like(left_face))
    right_face = jnp.where(column_tile < grid_cols - 1, right_face, jnp.zeros_like(right_face))
    widened = jnp.concatenate([left_face, tile_grid, right_face], axis=2)
    upper_face = neighbour(widened[:, -1:], grid_cols)
    lower_face = neighbour(widened[:, :1], -grid_cols)
    return jnp.concatenate([upper_face, widened, lower_face], axis=1)


def normalize(values, mean_channel, scale_channel, norm_gain, norm_bias):
    normed = (values.astype(jnp.float32) - mean_channel) * scale_channel * norm_gain + norm_bias
    return jax.nn.silu(normed)


def on_device(
    seq_rows, plan_owner, plan_slot, live_frames, norm_gain, norm_bias, conv_weight, conv_bias
):
    row_count, channels = seq_rows.shape
    out_width = conv_bias.shape[0]
    tile_count = lax.axis_size("tile")
    clip_count = lax.axis_size("clip")
    owner_count = tile_count * clip_count
    capacity = 3 * (row_count // owner_count) // 2
    per_group = channels // GROUPS
    plane_size = TH * TW
    voxel_total = float(plane_size * tile_count)
    row_index = jnp.arange(row_count, dtype=jnp.int32)
    owner_table = (plan_owner[:, None] == jnp.arange(owner_count, dtype=jnp.int32)[None, :]).astype(
        jnp.int32
    )
    ranking = jnp.sum((jnp.cumsum(owner_table, axis=0) - 1) * owner_table, axis=1)
    position = plan_owner * capacity + ranking
    my_clip = lax.axis_index("clip")
    my_tile = lax.axis_index("tile")
    frames_live = live_frames[my_clip]
    outgoing = (
        jnp.zeros((owner_count * capacity, channels), jnp.bfloat16).at[position].set(seq_rows)
    )
    slot_list = (
        jnp.full((owner_count * capacity,), row_count, jnp.int32).at[position].set(plan_slot)
    )
    outgoing = outgoing.reshape(clip_count, tile_count, capacity, channels)
    slot_list = slot_list.reshape(clip_count, tile_count, capacity)
    arrived, arrived_slots = (
        lax.all_to_all(
            lax.all_to_all(outgoing, "tile", split_axis=1, concat_axis=1, tiled=True),
            "clip",
            split_axis=0,
            concat_axis=0,
            tiled=True,
        ),
        lax.all_to_all(
            lax.all_to_all(slot_list, "tile", split_axis=1, concat_axis=1, tiled=True),
            "clip",
            split_axis=0,
            concat_axis=0,
            tiled=True,
        ),
    )
    tile_rows = (
        jnp.zeros((row_count, channels), jnp.bfloat16)
        .at[arrived_slots.reshape(-1)]
        .set(arrived.reshape(-1, channels), mode="drop")
    )
    grid_cols = GW
    grid_rows = tile_count // grid_cols
    column_tile = my_tile % grid_cols
    row_tile = my_tile // grid_cols
    live_frame = jnp.arange(LT) < frames_live
    values = tile_rows.astype(jnp.float32)
    live_row = (row_index // plane_size < frames_live).astype(jnp.float32)
    first_sum = jnp.dot(live_row, values, precision=HIGHEST).reshape(GROUPS, per_group).sum(axis=1)
    second_sum = (
        jnp.dot(live_row, values * values, precision=HIGHEST).reshape(GROUPS, per_group).sum(axis=1)
    )
    raw_padded = extend(tile_rows.reshape(LT, TH, TW, channels), column_tile, grid_cols)
    first_sum, second_sum = lax.psum((first_sum, second_sum), "tile")
    count_clip = per_group * frames_live.astype(jnp.float32) * voxel_total
    mean_group = first_sum / count_clip
    scale_group = lax.rsqrt(second_sum / count_clip - mean_group * mean_group + EPSILON)
    mean_channel = jnp.repeat(mean_group, per_group)
    scale_channel = jnp.repeat(scale_group, per_group)
    inside_rows = jnp.arange(TH + 2)
    inside_cols = jnp.arange(TW + 2)
    rows_inside = ((inside_rows > 0) | (row_tile > 0)) & (
        (inside_rows < TH + 1) | (row_tile < grid_rows - 1)
    )
    cols_inside = ((inside_cols > 0) | (column_tile > 0)) & (
        (inside_cols < TW + 1) | (column_tile < grid_cols - 1)
    )
    valid_mask = rows_inside[:, None] & cols_inside[None, :]
    activated = normalize(raw_padded, mean_channel, scale_channel, norm_gain, norm_bias)
    padded = jnp.where(valid_mask[None, :, :, None], activated, 0.0).astype(jnp.bfloat16)
    padded = jnp.concatenate(
        [jnp.zeros((2, TH + 2, TW + 2, channels), jnp.bfloat16), padded], axis=0
    )
    accumulated = jnp.zeros((LT, TH, TW, out_width), jnp.float32)
    for tap_t in range(3):
        for tap_h in range(3):
            slab_rows = padded[tap_t : tap_t + LT, tap_h : tap_h + TH].reshape(-1, channels)
            kernel = conv_weight[tap_t, tap_h].reshape(channels, 3 * out_width)
            product = jnp.dot(slab_rows, kernel, preferred_element_type=jnp.float32)
            product = product.reshape(LT, TH, TW + 2, 3, out_width)
            for tap_w in range(3):
                accumulated = accumulated + product[:, :, tap_w : tap_w + TW, tap_w]
    decoded = jnp.where(live_frame[:, None, None, None], accumulated + conv_bias, 0.0)
    return decoded.astype(jnp.bfloat16)[None, None]


def solution(mesh):
    return jax.shard_map(
        on_device,
        mesh=mesh,
        in_specs=(
            P(("tile", "clip"), None),
            P(("tile", "clip")),
            P(("tile", "clip")),
            P(),
            P(),
            P(),
            P(),
            P(),
        ),
        out_specs=P("clip", "tile", None, None, None, None),
        check_vma=False,
    )
```

profile of v0, /device:TPU:0, one launch (start us, length us, event | category | flops | bytes accessed | tf_op | source)
XLA Modules:
  0.0 185.9 jit_solution(9642833911319196824)
XLA Ops:
  0.7 9.0 %reduce-window.6 = s32[32,8,128]{2,1,0:T(8,128)S(1)} reduce-window(s32[32,8,128]{2,1,0:T(8,128)S(1)} %fusion.53, s32[]{:T(128)} %constant.69.clone.1), window={size=1x1x128 pad=0_0x0_0x127_0}, to_apply=%region_0.0 | reduce-window | flops 4161536 | bytes 262148 | tf_op jit(solution)/shard_map/reduce-window
  11.6 4.5 %scatter_custom_fusion = s32[1536]{0:T(1024)S(1)} fusion(s32[1024]{0:T(1024)S(1)} %compare_select_fusion.1, s32[1024]{0:T(1024)} %param.10, s32[]{:T(128)} %constant.80.clone.1), kind=kCustom, calls=%fused_computation.106 | custom fusion | bytes 6656 | tf_op jit(solution)/shard_map/scatter | solution.py:66
  16.9 7.3 %all-to-all-start = ((s32[8,1,192]{2,1,0:T(1,128)}), s32[8,1,192]{2,1,0:T(1,128)S(1)}, u32[]{:S(2)}, u32[]{:S(2)}) async-start(s32[8,1,192]{2,1,0:T(1,128)} %reshape.525), calls=%async_computation | async-start | bytes 16384 | tf_op jit(solution)/shard_map/all_to_all | solution.py:79
  24.1 6.0 %scatter_custom_fusion.1 = bf16[1536,512]{1,0:T(8,128)(2,1)S(1)} fusion(s32[1024]{0:T(1024)S(1)} %compare_select_fusion.1, bf16[1024,512]{1,0:T(8,128)(2,1)} %param.8, bf16[]{:T(256)} %constant.79.clone.1), kind=kCustom, calls=%fused_computation.80 | custom fusion | bytes 1573376 | tf_op jit(solution)/shard_map/scatter | solution.py:63
  30.2 1.3 copy.91
  31.5 6.0 %all-to-all-start.2 = ((bf16[4,8,48,512]{3,2,0,1:T(8,128)(2,1)}), bf16[4,8,48,512]{3,2,0,1:T(8,128)(2,1)S(1)}, u32[]{:S(2)}, u32[]{:S(2)}) async-start(bf16[4,8,48,512]{3,2,0,1:T(8,128)(2,1)} %copy.91), calls=%async_computation.2 | async-start | bytes 3145728 | tf_op jit(solution)/shard_map/all_to_all | solution.py:72
  39.4 34.5 %all-to-all-done.2 = bf16[4,8,48,512]{3,2,0,1:T(8,128)(2,1)S(1)} async-done(((bf16[4,8,48,512]{3,2,0,1:T(8,128)(2,1)}), bf16[4,8,48,512]{3,2,0,1:T(8,128)(2,1)S(1)}, u32[]{:S(2)}, u32[]{:S(2)}) %all-to-all-start.2) | async-done | bytes 1572896 | tf_op jit(solution)/shard_map/all_to_all | solution.py:72
  73.9 3.2 %all-to-all-start.1 = ((s32[4,1,384]{2,1,0:T(1,128)}), s32[4,1,384]{2,1,0:T(1,128)S(1)}, u32[]{:S(2)}, u32[]{:S(2)}) async-start(s32[4,1,384]{2,1,0:T(1,128)} %reshape.527), calls=%async_computation.1 | async-start | bytes 12288 | tf_op jit(solution)/shard_map/all_to_all | solution.py:78
  79.7 1.3 all-to-all-done.1
  81.0 4.3 %all-to-all-start.3 = ((bf16[4,8,48,512]{3,2,1,0:T(8,128)(2,1)}), bf16[4,8,48,512]{3,2,1,0:T(8,128)(2,1)}, u32[]{:S(2)}, u32[]{:S(2)}) async-start(bf16[4,8,48,512]{3,2,1,0:T(8,128)(2,1)} %copy.92), calls=%async_computation.3 | async-start | bytes 3145728 | tf_op jit(solution)/shard_map/all_to_all | solution.py:71
  85.9 5.5 %fusion.67 = (bf16[1,1,512,3,256]{4,2,3,1,0:T(8,128)(2,1)}, bf16[1,1,512,3,256]{4,2,3,1,0:T(8,128)(2,1)}, bf16[1,1,512,3,256]{4,2,3,1,0:T(8,128)(2,1)}, bf16[1,1...) fusion(bf16[3,3,512,3,256]{4,2,3,1,0:T(8,128)(2,1)} %param.14), kind=kLoop, calls=%fused_computation.122 | loop fusion | bytes 14155776 | tf_op jit(solution)/shard_map/slice | solution.py:127
  91.4 1.4 copy.130
  92.8 2.4 %copy.138 = bf16[1,1,512,3,256]{2,4,3,1,0:T(8,128)(2,1)} copy(bf16[1,1,512,3,256]{4,2,3,1,0:T(8,128)(2,1)} %get-tuple-element.10) | data formatting | bytes 1572864
  95.1 2.3 %copy.137 = bf16[1,1,512,3,256]{2,4,3,1,0:T(8,128)(2,1)} copy(bf16[1,1,512,3,256]{4,2,3,1,0:T(8,128)(2,1)} %get-tuple-element.11) | data formatting | bytes 1572864
  97.4 2.3 %copy.135 = bf16[1,1,512,3,256]{2,4,3,1,0:T(8,128)(2,1)} copy(bf16[1,1,512,3,256]{4,2,3,1,0:T(8,128)(2,1)} %get-tuple-element.12) | data formatting | bytes 1572864
  100.9 1.4 copy.133
  102.3 2.3 %copy.132 = bf16[1,1,512,3,256]{2,4,3,1,0:T(8,128)(2,1)} copy(bf16[1,1,512,3,256]{4,2,3,1,0:T(8,128)(2,1)} %get-tuple-element.15) | data formatting | bytes 1572864
  104.6 2.3 %copy.131 = bf16[1,1,512,3,256]{2,4,3,1,0:T(8,128)(2,1)} copy(bf16[1,1,512,3,256]{4,2,3,1,0:T(8,128)(2,1)} %get-tuple-element.16) | data formatting | bytes 1572864
  109.7 8.0 %scatter_custom_fusion.2 = bf16[1024,512]{1,0:T(8,128)(2,1)S(1)} fusion(s32[1536]{0:T(1024)S(1)} %fusion.54, bf16[1536,512]{1,0:T(8,128)(2,1)} %bitcast.5, bf16[]{:T(256)} %constant.79.clone.1), kind=kCustom, calls=%fused_computation.82 | custom fusion | bytes 1049088 | tf_op jit(solution)/shard_map/scatter | solution.py:89
  118.7 3.3 %collective-permute-start = (bf16[4,8,1,512]{3,2,1,0:T(2,128)(2,1)S(1)}, bf16[4,8,1,512]{3,2,1,0:T(2,128)(2,1)S(1)}, u32[]{:S(2)}, u32[]{:S(2)}) collective-permute-start(bf16[4,8,1,512]{3,2,1,0:T(2,128)(2,1)S(1)} %get-tuple-element.20), channel_id=1, source_target_pairs={{0,4},{4,8},{8,12},{12,16},{16,20},{20,24},{24,28},{1,5},{5,9},{9,... | collective-permute-start | bytes 98312 | tf_op jit(solution)/shard_map/ppermute | solution.py:18
  122.7 1.3 collective-permute-start.1
  124.0 20.7 %all-reduce.1 = (f32[32]{0:T(128)S(1)}, f32[32]{0:T(128)S(1)}) all-reduce(f32[32]{0:T(128)S(1)} %reduce_sum.28, f32[32]{0:T(128)S(1)} %reduce_sum.29), channel_id=1, replica_groups=mesh['tile'=8,'clip'=4] {'tile'}, use_global_device_ids=true, to_apply=%region_7.8 | all-reduce | flops 64 | bytes 512 | tf_op jit(solution)/shard_map/psum | solution.py:103
  145.0 1.3 collective-permute-start.2
  146.3 1.3 collective-permute-start.3
  149.1 6.4 %collective-permute-done.3 = bf16[4,1,34,512]{3,2,1,0:T(8,128)(2,1)S(1)} collective-permute-done((bf16[4,1,34,512]{3,2,1,0:T(8,128)(2,1)S(1)}, bf16[4,1,34,512]{3,2,1,0:T(8,128)(2,1)S(1)}, u32[]{:S(2)}, u32[]{:S(2)}) %collective-permute-start.3) | collective-permute-done | bytes 139296 | tf_op jit(solution)/shard_map/ppermute | solution.py:18
  155.5 2.5 %select_convert_fusion = bf16[4,10,34,512]{3,2,1,0:T(8,128)(2,1)S(1)} fusion(bf16[4,1,34,512]{3,2,1,0:T(8,128)(2,1)S(1)} %collective-permute-done.3, bf16[4,8,1,512]{3,2,1,0:T(2,128)(2,1)S(1)} %broadcast_select_fusion, bf16[4,8,32,512]{3,2,1,0:T(8,128)(2,1)S(1)} %bitcast.241, bf16[4,8,1,512]{3,2,1,0:T(2,128)(2,1)S(1)} %broadcast_select_fusion.1, ...), kind=kLoop, calls=%fused_computation.3 | loop fusion | flops 13926400 | bytes 2793812 | tf_op jit(solution)/shard_map/convert_element_type | solution.py:119
  158.0 2.5 %fusion.21 = f32[4,8,34,3,256]{4,2,1,0,3:T(8,128)S(1)} fusion(bf16[4,10,34,512]{3,2,1,0:T(8,128)(2,1)S(1)} %select_convert_fusion, bf16[1,1,512,3,256]{2,4,3,1,0:T(8,128)(2,1)} %copy.139), kind=kOutput, calls=%fused_computation.26 | convolution fusion | flops 855638016 | bytes 5439488 | tf_op jit(solution)/shard_map/dot_general | solution.py:128
  165.6 3.1 %fusion.19 = f32[4,8,34,3,256]{4,2,3,1,0:T(8,128)} fusion(bf16[4,10,34,512]{3,2,1,0:T(8,128)(2,1)S(1)} %select_convert_fusion, bf16[1,1,512,3,256]{2,4,3,1,0:T(8,128)(2,1)S(1)} %copy-done), kind=kOutput, calls=%fused_computation.24 | convolution fusion | flops 855638016 | bytes 5521408 | tf_op jit(solution)/shard_map/dot_general | solution.py:128
  168.7 3.2 %fusion.23 = f32[4,8,34,3,256]{4,2,1,0,3:T(8,128)} fusion(bf16[4,10,34,512]{3,2,1,0:T(8,128)(2,1)S(1)} %select_convert_fusion, bf16[1,1,512,3,256]{2,4,3,1,0:T(8,128)(2,1)S(1)} %copy-done.5), kind=kOutput, calls=%fused_computation.30 | convolution fusion | flops 855638016 | bytes 5439488 | tf_op jit(solution)/shard_map/dot_general | solution.py:128
  171.9 3.2 %fusion.22 = f32[4,8,34,3,256]{4,2,1,0,3:T(8,128)} fusion(bf16[4,10,34,512]{3,2,1,0:T(8,128)(2,1)S(1)} %select_convert_fusion, bf16[1,1,512,3,256]{2,4,3,1,0:T(8,128)(2,1)S(1)} %copy-done.4), kind=kOutput, calls=%fused_computation.28 | convolution fusion | flops 855638016 | bytes 5439488 | tf_op jit(solution)/shard_map/dot_general | solution.py:128
  175.1 3.2 %fusion.4 = f32[4,8,34,3,256]{4,2,3,1,0:T(8,128)} fusion(bf16[4,10,34,512]{3,2,1,0:T(8,128)(2,1)S(1)} %select_convert_fusion, bf16[1,1,512,3,256]{2,4,3,1,0:T(8,128)(2,1)S(1)} %copy.130), kind=kOutput, calls=%fused_computation.14 | convolution fusion | flops 855638016 | bytes 5521408 | tf_op jit(solution)/shard_map/dot_general | solution.py:128
  178.3 7.6 %fusion.27 = bf16[1,1,4,8,32,256]{5,4,3,2,1,0:T(8,128)(2,1)} fusion(f32[4,8,34,3,256]{4,2,1,0,3:T(8,128)S(1)} %fusion.21, f32[4,8,34,3,256]{4,2,1,0,3:T(8,128)} %fusion.22, f32[4,8,34,3,256]{4,2,1,0,3:T(8,128)} %fusion.23, f32[4,8,34,3,256]{4,2,3,1,0:T(8,128)} %fusion.19, f32[4,8,34,3,256]{4,2,3,1,0:T(8,128)S(1)} %fusion.16, ...), kind=kLoop, calls=%fused_computation.35 | loop fusion | flops 7602176 | bytes 28836868 | tf_op jit(solution)/shard_map/convert_element_type | solution.py:133
  (75 shorter events, 20.1 us)
Async XLA Ops:
  16.9 14.6 %all-to-all-start = ((s32[8,1,192]{2,1,0:T(1,128)}), s32[8,1,192]{2,1,0:T(1,128)S(1)}, u32[]{:S(2)}, u32[]{:S(2)}) async-start(s32[8,1,192]{2,1,0:T(1,128)} %reshape.525), calls=%async_computation | async-start | bytes 16384 | tf_op jit(solution)/shard_map/all_to_all | solution.py:79
  30.2 47.0 %copy-start.9 = (s32[4]{0:T(128)S(1)}, s32[4]{0:T(128)}, u32[]{:S(2)}) copy-start(s32[4]{0:T(128)} %param.11) | copy-start | bytes 52
  31.5 42.4 %all-to-all-start.2 = ((bf16[4,8,48,512]{3,2,0,1:T(8,128)(2,1)}), bf16[4,8,48,512]{3,2,0,1:T(8,128)(2,1)S(1)}, u32[]{:S(2)}, u32[]{:S(2)}) async-start(bf16[4,8,48,512]{3,2,0,1:T(8,128)(2,1)} %copy.91), calls=%async_computation.2 | async-start | bytes 3145728 | tf_op jit(solution)/shard_map/all_to_all | solution.py:72
  73.9 7.0 %all-to-all-start.1 = ((s32[4,1,384]{2,1,0:T(1,128)}), s32[4,1,384]{2,1,0:T(1,128)S(1)}, u32[]{:S(2)}, u32[]{:S(2)}) async-start(s32[4,1,384]{2,1,0:T(1,128)} %reshape.527), calls=%async_computation.1 | async-start | bytes 12288 | tf_op jit(solution)/shard_map/all_to_all | solution.py:78
  81.0 28.7 %all-to-all-start.3 = ((bf16[4,8,48,512]{3,2,1,0:T(8,128)(2,1)}), bf16[4,8,48,512]{3,2,1,0:T(8,128)(2,1)}, u32[]{:S(2)}, u32[]{:S(2)}) async-start(bf16[4,8,48,512]{3,2,1,0:T(8,128)(2,1)} %copy.92), calls=%async_computation.3 | async-start | bytes 3145728 | tf_op jit(solution)/shard_map/all_to_all | solution.py:71
  109.7 45.9 %copy-start.6 = (f32[512]{0:T(512)S(1)}, f32[512]{0:T(512)}, u32[]{:S(2)}) copy-start(f32[512]{0:T(512)} %param.13) | copy-start | bytes 6148
  109.7 45.9 %copy-start.7 = (f32[512]{0:T(512)S(1)}, f32[512]{0:T(512)}, u32[]{:S(2)}) copy-start(f32[512]{0:T(512)} %param.12) | copy-start | bytes 6148
  118.7 26.0 %collective-permute-start = (bf16[4,8,1,512]{3,2,1,0:T(2,128)(2,1)S(1)}, bf16[4,8,1,512]{3,2,1,0:T(2,128)(2,1)S(1)}, u32[]{:S(2)}, u32[]{:S(2)}) collective-permute-start(bf16[4,8,1,512]{3,2,1,0:T(2,128)(2,1)S(1)} %get-tuple-element.20), channel_id=1, source_target_pairs={{0,4},{4,8},{8,12},{12,16},{16,20},{20,24},{24,28},{1,5},{5,9},{9,... | collective-permute-start | bytes 98312 | tf_op jit(solution)/shard_map/ppermute | solution.py:18
  122.7 22.1 %collective-permute-start.1 = (bf16[4,8,1,512]{3,2,1,0:T(2,128)(2,1)S(1)}, bf16[4,8,1,512]{3,2,1,0:T(2,128)(2,1)S(1)}, u32[]{:S(2)}, u32[]{:S(2)}) collective-permute-start(bf16[4,8,1,512]{3,2,1,0:T(2,128)(2,1)S(1)} %get-tuple-element.21), channel_id=1, source_target_pairs={{4,0},{8,4},{12,8},{16,12},{20,16},{24,20},{28,24},{5,1},{9,5},{13... | collective-permute-start | bytes 98312 | tf_op jit(solution)/shard_map/ppermute | solution.py:18
  145.0 4.2 %collective-permute-start.2 = (bf16[4,1,34,512]{3,2,1,0:T(8,128)(2,1)S(1)}, bf16[4,1,34,512]{3,2,1,0:T(8,128)(2,1)S(1)}, u32[]{:S(2)}, u32[]{:S(2)}) collective-permute-start(bf16[4,1,34,512]{3,2,1,0:T(8,128)(2,1)S(1)} %get-tuple-element.18), channel_id=1, source_target_pairs={{0,16},{4,20},{8,24},{12,28},{1,17},{5,21},{9,25},{13,29},{2,18},{... | collective-permute-start | bytes 417800 | tf_op jit(solution)/shard_map/ppermute | solution.py:18
  146.3 9.2 %collective-permute-start.3 = (bf16[4,1,34,512]{3,2,1,0:T(8,128)(2,1)S(1)}, bf16[4,1,34,512]{3,2,1,0:T(8,128)(2,1)S(1)}, u32[]{:S(2)}, u32[]{:S(2)}) collective-permute-start(bf16[4,1,34,512]{3,2,1,0:T(8,128)(2,1)S(1)} %get-tuple-element.19), channel_id=1, source_target_pairs={{16,0},{20,4},{24,8},{28,12},{17,1},{21,5},{25,9},{29,13},{18,2},{... | collective-permute-start | bytes 417800 | tf_op jit(solution)/shard_map/ppermute | solution.py:18
  158.0 2.5 %copy-start.3 = (bf16[1,1,512,3,256]{2,4,3,1,0:T(8,128)(2,1)S(1)}, bf16[1,1,512,3,256]{2,4,3,1,0:T(8,128)(2,1)}, u32[]{:S(2)}) copy-start(bf16[1,1,512,3,256]{2,4,3,1,0:T(8,128)(2,1)} %copy.131) | copy-start | bytes 2359300
  160.5 1.3 copy-start.2
  163.0 1.3 copy-start.1
  164.3 1.3 copy-start
  165.6 3.2 %copy-start.5 = (bf16[1,1,512,3,256]{2,4,3,1,0:T(8,128)(2,1)S(1)}, bf16[1,1,512,3,256]{2,4,3,1,0:T(8,128)(2,1)}, u32[]{:S(2)}) copy-start(bf16[1,1,512,3,256]{2,4,3,1,0:T(8,128)(2,1)} %copy.137) | copy-start | bytes 2359300
  168.7 3.2 %copy-start.4 = (bf16[1,1,512,3,256]{2,4,3,1,0:T(8,128)(2,1)S(1)}, bf16[1,1,512,3,256]{2,4,3,1,0:T(8,128)(2,1)}, u32[]{:S(2)}) copy-start(bf16[1,1,512,3,256]{2,4,3,1,0:T(8,128)(2,1)} %copy.138) | copy-start | bytes 2359300
  175.1 3.2 %copy-start.8 = (f32[256]{0:T(256)S(1)}, f32[256]{0:T(256)}, u32[]{:S(2)}) copy-start(f32[256]{0:T(256)} %param.15) | copy-start | bytes 3076
where the time goes:
time: 187 us; the launch traced here: 186 us
  local copies, waits for them, and re-layouts  47 us (25%)
  waiting for transfers between devices  43.4 us (23%)
  starting transfers between devices  28.1 us (15%)
  other arithmetic  24.4 us (13%)
  matrix products  21.3 us (11%)
  blocking collectives  20.7 us (11%)
    all_to_all x1, waiting for transfers between devices, on_device(): lax.all_to_all(outgoing, 'tile', split_axis=1, concat_axis=1, tiled=True)  34.5 us
    psum x1, blocking collectives, on_device(): first_sum, second_sum = lax.psum((first_sum, second_sum), 'tile')  20.7 us
    dot_general x9, matrix products, on_device(): product = jnp.dot(slab_rows, kernel, preferred_element_type=jnp.float32)  20.2 us
    unnamed x33, local copies, waits for them, and re-layouts  18.3 us
    another operation x2, other arithmetic  9.04 us
    scatter x1, local copies, waits for them, and re-layouts, on_device(): tile_rows = jnp.zeros((row_count, channels), jnp.bfloat16).at[arrived_slo...  8 us
    ppermute x4, waiting for transfers between devices, shifted(): return lax.ppermute(block, axis, route)  7.63 us
    convert_element_type x1, other arithmetic, on_device(): return decoded.astype(jnp.bfloat16)[None, None]  7.58 us
  transfers between devices with their start and end apart: 8, of which 4 were waited for; matrix products, arithmetic and copies ran while one was open for 20% of the time, Pallas kernels for 0%

commit v1 on v0

--- a/solution.py
+++ b/solution.py
@@ -76,7 +76,12 @@
             tiled=True,
         ),
         lax.all_to_all(
-            lax.all_to_all(slot_list, "tile", split_axis=1, concat_axis=1, tiled=True),
+            jnp.concatenate(
+                lax.all_to_all(
+                    jnp.stack(jnp.split(slot_list, lax.axis_size("tile"), axis=1)), "tile", 0, 0
+                ),
+                axis=1,
+            ),
             "clip",
             split_axis=0,
             concat_axis=0,

time: 187 us -> 187 us (level)
    unnamed x33 -> x40, local copies, waits for them, and re-layouts: 18.3 us -> 18.4 us
where the time goes in v1:
time: 187 us; the launch traced here: 186 us
  local copies, waits for them, and re-layouts  47.1 us (25%)
  waiting for transfers between devices  43.4 us (23%)
  starting transfers between devices  28.2 us (15%)
  other arithmetic  24.4 us (13%)
  matrix products  21.3 us (11%)
  blocking collectives  20.7 us (11%)
    all_to_all x1, waiting for transfers between devices, on_device(): lax.all_to_all(outgoing, 'tile', split_axis=1, concat_axis=1, tiled=True)  34.5 us
    psum x1, blocking collectives, on_device(): first_sum, second_sum = lax.psum((first_sum, second_sum), 'tile')  20.7 us
    dot_general x9, matrix products, on_device(): product = jnp.dot(slab_rows, kernel, preferred_element_type=jnp.float32)  20.1 us
    unnamed x40, local copies, waits for them, and re-layouts  18.4 us
    another operation x2, other arithmetic  9.04 us
    scatter x1, local copies, waits for them, and re-layouts, on_device(): tile_rows = jnp.zeros((row_count, channels), jnp.bfloat16).at[arrived_slo...  8 us
    ppermute x4, waiting for transfers between devices, shifted(): return lax.ppermute(block, axis, route)  7.63 us
    convert_element_type x1, other arithmetic, on_device(): return decoded.astype(jnp.bfloat16)[None, None]  7.58 us
  transfers between devices with their start and end apart: 8, of which 4 were waited for; matrix products, arithmetic and copies ran while one was open for 20% of the time, Pallas kernels for 0%

profile of v1, /device:TPU:0, one launch (start us, length us, event | category | flops | bytes accessed | tf_op | source)
XLA Modules:
  0.0 186.1 jit_solution(14362057971189687317)
XLA Ops:
  0.7 9.0 %reduce-window.6 = s32[32,8,128]{2,1,0:T(8,128)S(1)} reduce-window(s32[32,8,128]{2,1,0:T(8,128)S(1)} %fusion.53, s32[]{:T(128)} %constant.69.clone.1), window={size=1x1x128 pad=0_0x0_0x127_0}, to_apply=%region_0.0 | reduce-window | flops 4161536 | bytes 262148 | tf_op jit(solution)/shard_map/reduce-window
  11.6 4.5 %scatter_custom_fusion = s32[1536]{0:T(1024)S(1)} fusion(s32[1024]{0:T(1024)S(1)} %compare_select_fusion.1, s32[1024]{0:T(1024)} %param.10, s32[]{:T(128)} %constant.80.clone.1), kind=kCustom, calls=%fused_computation.114 | custom fusion | bytes 6656 | tf_op jit(solution)/shard_map/scatter | solution.py:66
  17.0 7.3 %all-to-all-start = ((s32[8,1,192]{2,1,0:T(1,128)}), s32[8,1,192]{2,1,0:T(1,128)S(1)}, u32[]{:S(2)}, u32[]{:S(2)}) async-start(s32[8,1,192]{2,1,0:T(1,128)} %reshape.533), calls=%async_computation | async-start | bytes 16384 | tf_op jit(solution)/shard_map/all_to_all | solution.py:80
  24.2 6.0 %scatter_custom_fusion.1 = bf16[1536,512]{1,0:T(8,128)(2,1)S(1)} fusion(s32[1024]{0:T(1024)S(1)} %compare_select_fusion.1, bf16[1024,512]{1,0:T(8,128)(2,1)} %param.8, bf16[]{:T(256)} %constant.79.clone.1), kind=kCustom, calls=%fused_computation.80 | custom fusion | bytes 1573376 | tf_op jit(solution)/shard_map/scatter | solution.py:63
  30.3 1.3 copy.123
  31.6 6.1 %all-to-all-start.2 = ((bf16[4,8,48,512]{3,2,0,1:T(8,128)(2,1)}), bf16[4,8,48,512]{3,2,0,1:T(8,128)(2,1)S(1)}, u32[]{:S(2)}, u32[]{:S(2)}) async-start(bf16[4,8,48,512]{3,2,0,1:T(8,128)(2,1)} %copy.123), calls=%async_computation.2 | async-start | bytes 3145728 | tf_op jit(solution)/shard_map/all_to_all | solution.py:72
  39.7 34.5 %all-to-all-done.2 = bf16[4,8,48,512]{3,2,0,1:T(8,128)(2,1)S(1)} async-done(((bf16[4,8,48,512]{3,2,0,1:T(8,128)(2,1)}), bf16[4,8,48,512]{3,2,0,1:T(8,128)(2,1)S(1)}, u32[]{:S(2)}, u32[]{:S(2)}) %all-to-all-start.2) | async-done | bytes 1572896 | tf_op jit(solution)/shard_map/all_to_all | solution.py:72
  74.2 3.2 %all-to-all-start.1 = ((s32[4,1,384]{2,1,0:T(1,128)}), s32[4,1,384]{2,1,0:T(1,128)S(1)}, u32[]{:S(2)}, u32[]{:S(2)}) async-start(s32[4,1,384]{2,1,0:T(1,128)} %reshape.535), calls=%async_computation.1 | async-start | bytes 12288 | tf_op jit(solution)/shard_map/all_to_all | solution.py:78
  79.9 1.3 all-to-all-done.1
  81.2 4.3 %all-to-all-start.3 = ((bf16[4,8,48,512]{3,2,1,0:T(8,128)(2,1)}), bf16[4,8,48,512]{3,2,1,0:T(8,128)(2,1)}, u32[]{:S(2)}, u32[]{:S(2)}) async-start(bf16[4,8,48,512]{3,2,1,0:T(8,128)(2,1)} %copy.124), calls=%async_computation.3 | async-start | bytes 3145728 | tf_op jit(solution)/shard_map/all_to_all | solution.py:71
  86.1 5.5 %fusion.67 = (bf16[1,1,512,3,256]{4,2,3,1,0:T(8,128)(2,1)}, bf16[1,1,512,3,256]{4,2,3,1,0:T(8,128)(2,1)}, bf16[1,1,512,3,256]{4,2,3,1,0:T(8,128)(2,1)}, bf16[1,1...) fusion(bf16[3,3,512,3,256]{4,2,3,1,0:T(8,128)(2,1)} %param.14), kind=kLoop, calls=%fused_computation.130 | loop fusion | bytes 14155776 | tf_op jit(solution)/shard_map/slice | solution.py:132
  91.6 1.4 copy.169
  93.0 2.4 %copy.177 = bf16[1,1,512,3,256]{2,4,3,1,0:T(8,128)(2,1)} copy(bf16[1,1,512,3,256]{4,2,3,1,0:T(8,128)(2,1)} %get-tuple-element.10) | data formatting | bytes 1572864
  95.4 2.3 %copy.176 = bf16[1,1,512,3,256]{2,4,3,1,0:T(8,128)(2,1)} copy(bf16[1,1,512,3,256]{4,2,3,1,0:T(8,128)(2,1)} %get-tuple-element.11) | data formatting | bytes 1572864
  97.7 2.3 %copy.174 = bf16[1,1,512,3,256]{2,4,3,1,0:T(8,128)(2,1)} copy(bf16[1,1,512,3,256]{4,2,3,1,0:T(8,128)(2,1)} %get-tuple-element.12) | data formatting | bytes 1572864
  101.1 1.4 copy.172
  102.5 2.3 %copy.171 = bf16[1,1,512,3,256]{2,4,3,1,0:T(8,128)(2,1)} copy(bf16[1,1,512,3,256]{4,2,3,1,0:T(8,128)(2,1)} %get-tuple-element.15) | data formatting | bytes 1572864
  104.8 2.3 %copy.170 = bf16[1,1,512,3,256]{2,4,3,1,0:T(8,128)(2,1)} copy(bf16[1,1,512,3,256]{4,2,3,1,0:T(8,128)(2,1)} %get-tuple-element.16) | data formatting | bytes 1572864
  109.9 8.0 %scatter_custom_fusion.2 = bf16[1024,512]{1,0:T(8,128)(2,1)S(1)} fusion(s32[1536]{0:T(1024)S(1)} %fusion.54, bf16[1536,512]{1,0:T(8,128)(2,1)} %bitcast.15, bf16[]{:T(256)} %constant.79.clone.1), kind=kCustom, calls=%fused_computation.82 | custom fusion | bytes 1049088 | tf_op jit(solution)/shard_map/scatter | solution.py:94
  118.9 3.3 %collective-permute-start = (bf16[4,8,1,512]{3,2,1,0:T(2,128)(2,1)S(1)}, bf16[4,8,1,512]{3,2,1,0:T(2,128)(2,1)S(1)}, u32[]{:S(2)}, u32[]{:S(2)}) collective-permute-start(bf16[4,8,1,512]{3,2,1,0:T(2,128)(2,1)S(1)} %get-tuple-element.20), channel_id=1, source_target_pairs={{0,4},{4,8},{8,12},{12,16},{16,20},{20,24},{24,28},{1,5},{5,9},{9,... | collective-permute-start | bytes 98312 | tf_op jit(solution)/shard_map/ppermute | solution.py:18
  122.9 1.3 collective-permute-start.1
  124.2 20.7 %all-reduce.1 = (f32[32]{0:T(128)S(1)}, f32[32]{0:T(128)S(1)}) all-reduce(f32[32]{0:T(128)S(1)} %reduce_sum.28, f32[32]{0:T(128)S(1)} %reduce_sum.29), channel_id=1, replica_groups=mesh['tile'=8,'clip'=4] {'tile'}, use_global_device_ids=true, to_apply=%region_7.8 | all-reduce | flops 64 | bytes 512 | tf_op jit(solution)/shard_map/psum | solution.py:108
  145.2 1.3 collective-permute-start.2
  146.5 1.3 collective-permute-start.3
  149.4 6.4 %collective-permute-done.3 = bf16[4,1,34,512]{3,2,1,0:T(8,128)(2,1)S(1)} collective-permute-done((bf16[4,1,34,512]{3,2,1,0:T(8,128)(2,1)S(1)}, bf16[4,1,34,512]{3,2,1,0:T(8,128)(2,1)S(1)}, u32[]{:S(2)}, u32[]{:S(2)}) %collective-permute-start.3) | collective-permute-done | bytes 139296 | tf_op jit(solution)/shard_map/ppermute | solution.py:18
  155.8 2.5 %select_convert_fusion = bf16[4,10,34,512]{3,2,1,0:T(8,128)(2,1)S(1)} fusion(bf16[4,1,34,512]{3,2,1,0:T(8,128)(2,1)S(1)} %collective-permute-done.3, bf16[4,8,1,512]{3,2,1,0:T(2,128)(2,1)S(1)} %broadcast_select_fusion, bf16[4,8,32,512]{3,2,1,0:T(8,128)(2,1)S(1)} %bitcast.266, bf16[4,8,1,512]{3,2,1,0:T(2,128)(2,1)S(1)} %broadcast_select_fusion.1, ...), kind=kLoop, calls=%fused_computation.3 | loop fusion | flops 13926400 | bytes 2793812 | tf_op jit(solution)/shard_map/convert_element_type | solution.py:124
  158.3 2.5 %fusion.21 = f32[4,8,34,3,256]{4,2,1,0,3:T(8,128)S(1)} fusion(bf16[4,10,34,512]{3,2,1,0:T(8,128)(2,1)S(1)} %select_convert_fusion, bf16[1,1,512,3,256]{2,4,3,1,0:T(8,128)(2,1)} %copy.178), kind=kOutput, calls=%fused_computation.26 | convolution fusion | flops 855638016 | bytes 5439488 | tf_op jit(solution)/shard_map/dot_general | solution.py:133
  165.8 3.1 %fusion.19 = f32[4,8,34,3,256]{4,2,3,1,0:T(8,128)} fusion(bf16[4,10,34,512]{3,2,1,0:T(8,128)(2,1)S(1)} %select_convert_fusion, bf16[1,1,512,3,256]{2,4,3,1,0:T(8,128)(2,1)S(1)} %copy-done), kind=kOutput, calls=%fused_computation.24 | convolution fusion | flops 855638016 | bytes 5521408 | tf_op jit(solution)/shard_map/dot_general | solution.py:133
  168.9 3.1 %fusion.23 = f32[4,8,34,3,256]{4,2,1,0,3:T(8,128)} fusion(bf16[4,10,34,512]{3,2,1,0:T(8,128)(2,1)S(1)} %select_convert_fusion, bf16[1,1,512,3,256]{2,4,3,1,0:T(8,128)(2,1)S(1)} %copy-done.5), kind=kOutput, calls=%fused_computation.30 | convolution fusion | flops 855638016 | bytes 5439488 | tf_op jit(solution)/shard_map/dot_general | solution.py:133
  172.1 3.2 %fusion.22 = f32[4,8,34,3,256]{4,2,1,0,3:T(8,128)} fusion(bf16[4,10,34,512]{3,2,1,0:T(8,128)(2,1)S(1)} %select_convert_fusion, bf16[1,1,512,3,256]{2,4,3,1,0:T(8,128)(2,1)S(1)} %copy-done.4), kind=kOutput, calls=%fused_computation.28 | convolution fusion | flops 855638016 | bytes 5439488 | tf_op jit(solution)/shard_map/dot_general | solution.py:133
  175.3 3.2 %fusion.4 = f32[4,8,34,3,256]{4,2,3,1,0:T(8,128)} fusion(bf16[4,10,34,512]{3,2,1,0:T(8,128)(2,1)S(1)} %select_convert_fusion, bf16[1,1,512,3,256]{2,4,3,1,0:T(8,128)(2,1)S(1)} %copy.169), kind=kOutput, calls=%fused_computation.14 | convolution fusion | flops 855638016 | bytes 5521408 | tf_op jit(solution)/shard_map/dot_general | solution.py:133
  178.5 7.6 %fusion.27 = bf16[1,1,4,8,32,256]{5,4,3,2,1,0:T(8,128)(2,1)} fusion(f32[4,8,34,3,256]{4,2,1,0,3:T(8,128)S(1)} %fusion.21, f32[4,8,34,3,256]{4,2,1,0,3:T(8,128)} %fusion.22, f32[4,8,34,3,256]{4,2,1,0,3:T(8,128)} %fusion.23, f32[4,8,34,3,256]{4,2,3,1,0:T(8,128)} %fusion.19, f32[4,8,34,3,256]{4,2,3,1,0:T(8,128)S(1)} %fusion.16, ...), kind=kLoop, calls=%fused_computation.35 | loop fusion | flops 7602176 | bytes 28836868 | tf_op jit(solution)/shard_map/convert_element_type | solution.py:138
  (84 shorter events, 20.1 us)
Async XLA Ops:
  17.0 14.6 %all-to-all-start = ((s32[8,1,192]{2,1,0:T(1,128)}), s32[8,1,192]{2,1,0:T(1,128)S(1)}, u32[]{:S(2)}, u32[]{:S(2)}) async-start(s32[8,1,192]{2,1,0:T(1,128)} %reshape.533), calls=%async_computation | async-start | bytes 16384 | tf_op jit(solution)/shard_map/all_to_all | solution.py:80
  31.6 45.9 %copy-start.9 = (s32[4]{0:T(128)S(1)}, s32[4]{0:T(128)}, u32[]{:S(2)}) copy-start(s32[4]{0:T(128)} %param.11) | copy-start | bytes 52
  31.6 42.6 %all-to-all-start.2 = ((bf16[4,8,48,512]{3,2,0,1:T(8,128)(2,1)}), bf16[4,8,48,512]{3,2,0,1:T(8,128)(2,1)S(1)}, u32[]{:S(2)}, u32[]{:S(2)}) async-start(bf16[4,8,48,512]{3,2,0,1:T(8,128)(2,1)} %copy.123), calls=%async_computation.2 | async-start | bytes 3145728 | tf_op jit(solution)/shard_map/all_to_all | solution.py:72
  74.2 7.0 %all-to-all-start.1 = ((s32[4,1,384]{2,1,0:T(1,128)}), s32[4,1,384]{2,1,0:T(1,128)S(1)}, u32[]{:S(2)}, u32[]{:S(2)}) async-start(s32[4,1,384]{2,1,0:T(1,128)} %reshape.535), calls=%async_computation.1 | async-start | bytes 12288 | tf_op jit(solution)/shard_map/all_to_all | solution.py:78
  81.2 28.7 %all-to-all-start.3 = ((bf16[4,8,48,512]{3,2,1,0:T(8,128)(2,1)}), bf16[4,8,48,512]{3,2,1,0:T(8,128)(2,1)}, u32[]{:S(2)}, u32[]{:S(2)}) async-start(bf16[4,8,48,512]{3,2,1,0:T(8,128)(2,1)} %copy.124), calls=%async_computation.3 | async-start | bytes 3145728 | tf_op jit(solution)/shard_map/all_to_all | solution.py:71
  109.9 45.9 %copy-start.6 = (f32[512]{0:T(512)S(1)}, f32[512]{0:T(512)}, u32[]{:S(2)}) copy-start(f32[512]{0:T(512)} %param.13) | copy-start | bytes 6148
  109.9 45.9 %copy-start.7 = (f32[512]{0:T(512)S(1)}, f32[512]{0:T(512)}, u32[]{:S(2)}) copy-start(f32[512]{0:T(512)} %param.12) | copy-start | bytes 6148
  118.9 26.0 %collective-permute-start = (bf16[4,8,1,512]{3,2,1,0:T(2,128)(2,1)S(1)}, bf16[4,8,1,512]{3,2,1,0:T(2,128)(2,1)S(1)}, u32[]{:S(2)}, u32[]{:S(2)}) collective-permute-start(bf16[4,8,1,512]{3,2,1,0:T(2,128)(2,1)S(1)} %get-tuple-element.20), channel_id=1, source_target_pairs={{0,4},{4,8},{8,12},{12,16},{16,20},{20,24},{24,28},{1,5},{5,9},{9,... | collective-permute-start | bytes 98312 | tf_op jit(solution)/shard_map/ppermute | solution.py:18
  122.9 22.1 %collective-permute-start.1 = (bf16[4,8,1,512]{3,2,1,0:T(2,128)(2,1)S(1)}, bf16[4,8,1,512]{3,2,1,0:T(2,128)(2,1)S(1)}, u32[]{:S(2)}, u32[]{:S(2)}) collective-permute-start(bf16[4,8,1,512]{3,2,1,0:T(2,128)(2,1)S(1)} %get-tuple-element.21), channel_id=1, source_target_pairs={{4,0},{8,4},{12,8},{16,12},{20,16},{24,20},{28,24},{5,1},{9,5},{13... | collective-permute-start | bytes 98312 | tf_op jit(solution)/shard_map/ppermute | solution.py:18
  145.2 4.2 %collective-permute-start.2 = (bf16[4,1,34,512]{3,2,1,0:T(8,128)(2,1)S(1)}, bf16[4,1,34,512]{3,2,1,0:T(8,128)(2,1)S(1)}, u32[]{:S(2)}, u32[]{:S(2)}) collective-permute-start(bf16[4,1,34,512]{3,2,1,0:T(8,128)(2,1)S(1)} %get-tuple-element.18), channel_id=1, source_target_pairs={{0,16},{4,20},{8,24},{12,28},{1,17},{5,21},{9,25},{13,29},{2,18},{... | collective-permute-start | bytes 417800 | tf_op jit(solution)/shard_map/ppermute | solution.py:18
  146.5 9.2 %collective-permute-start.3 = (bf16[4,1,34,512]{3,2,1,0:T(8,128)(2,1)S(1)}, bf16[4,1,34,512]{3,2,1,0:T(8,128)(2,1)S(1)}, u32[]{:S(2)}, u32[]{:S(2)}) collective-permute-start(bf16[4,1,34,512]{3,2,1,0:T(8,128)(2,1)S(1)} %get-tuple-element.19), channel_id=1, source_target_pairs={{16,0},{20,4},{24,8},{28,12},{17,1},{21,5},{25,9},{29,13},{18,2},{... | collective-permute-start | bytes 417800 | tf_op jit(solution)/shard_map/ppermute | solution.py:18
  158.3 2.5 %copy-start.3 = (bf16[1,1,512,3,256]{2,4,3,1,0:T(8,128)(2,1)S(1)}, bf16[1,1,512,3,256]{2,4,3,1,0:T(8,128)(2,1)}, u32[]{:S(2)}) copy-start(bf16[1,1,512,3,256]{2,4,3,1,0:T(8,128)(2,1)} %copy.170) | copy-start | bytes 2359300
  160.7 1.3 copy-start.2
  163.3 1.3 copy-start.1
  164.5 1.3 copy-start
  165.8 3.1 %copy-start.5 = (bf16[1,1,512,3,256]{2,4,3,1,0:T(8,128)(2,1)S(1)}, bf16[1,1,512,3,256]{2,4,3,1,0:T(8,128)(2,1)}, u32[]{:S(2)}) copy-start(bf16[1,1,512,3,256]{2,4,3,1,0:T(8,128)(2,1)} %copy.176) | copy-start | bytes 2359300
  168.9 3.1 %copy-start.4 = (bf16[1,1,512,3,256]{2,4,3,1,0:T(8,128)(2,1)S(1)}, bf16[1,1,512,3,256]{2,4,3,1,0:T(8,128)(2,1)}, u32[]{:S(2)}) copy-start(bf16[1,1,512,3,256]{2,4,3,1,0:T(8,128)(2,1)} %copy.177) | copy-start | bytes 2359300
  175.3 3.2 %copy-start.8 = (f32[256]{0:T(256)S(1)}, f32[256]{0:T(256)}, u32[]{:S(2)}) copy-start(f32[256]{0:T(256)} %param.15) | copy-start | bytes 3076
